TPU v7x, 32 devices: a whole 2x2x4 slice. The times are simulated.
32 devices in a mesh: gx: 2 (over y), gy: 4 (over z), gz: 4 (over x, core).
Axes of the slice: x: 2, y: 2, z: 4, core: 2. Of those that a mesh axis runs over, the one named last changes fastest.
Arguments:
- features: bfloat16 [64, 2, 4, 8192], P(None, 'gx', 'gy', 'gz'), may hold values from -6 to 6
- tiles: bfloat16 [2, 4, 128, 64, 512], P('gx', 'gy', 'gz'), may hold values from -0.25 to 0.25
- scales: float32 [2, 4, 128, 8], P('gx', 'gy', 'gz'), may hold values from 0.5 to 2
- slots: int32 [2, 4, 128, 8], P('gx', 'gy', 'gz'), may hold values from 0 to 175, as said below
- live: int32 [2, 4, 128], P('gx', 'gy', 'gz'), may hold values from 2 to 8, as said below
- times: float32 [64], replicated, may hold values from 0.6 to 1.6
Outputs:
- diffused: bfloat16 [64, 2, 4, 8192], P(None, 'gx', 'gy', 'gz')
Inputs may be any that keep to these rules, and one draw needn't show every extreme that they name: Slot 0 of every block row is the row's own block; slots 1 to 3 hold blocks of the row's own device, the others blocks from the shared set. `live`: each device has some block row with all 8 slots used.
All inputs are finite; a program needn't handle non-finite values.
Results may differ from a plain program's by a relative error of at most 0.0032.
Values may be sent and summed in bfloat16 or wider, within the bound.
No kernel may reach another device: no remote copies, remote signals or barrier semaphores. Data moves between devices by JAX's collectives and lax.ppermute only.
A program may use at most 64 MiB of HBM per device.

v0:
```python
import jax
import jax.numpy as jnp
from jax import lax
from jax.sharding import PartitionSpec as P

PB = 64
TERMS = 3


def with_halo(cells, sides, width):
    for axis, dim in sides:
        count = lax.axis_size(axis)
        ends = count - 1
        head = lax.slice_in_dim(cells, 0, width, axis=dim)
        tail = lax.slice_in_dim(cells, cells.shape[dim] - width, cells.shape[dim], axis=dim)
        cells = jnp.concatenate(
            [
                lax.ppermute(tail, axis, [(i, (i + 1) % count) for i in range(ends)]),
                cells,
                lax.ppermute(head, axis, [((i + 1) % count, i) for i in range(ends)]),
            ],
            axis=dim,
        )
    return cells


def to_blocks(value):
    count = value.shape[3] // PB
    return (
        value.reshape(value.shape[0], count, PB)
        .transpose(1, 0, 2)
        .reshape(count, value.shape[0] * PB)
    )


def shared_blocks(rim_rows):
    width = rim_rows.shape[1]
    panel = lax.all_gather(rim_rows, "gz", axis=0, tiled=True)
    grid = with_halo(panel.reshape(1, 1, panel.shape[0], width), (("gx", 0), ("gy", 1)), 1)
    return grid.reshape(-1, width)


def apply_operator(value, tile_rows, scale_rows, slot_rows, live_rows):
    blocks = to_blocks(value)
    count = blocks.shape[0]
    slot_count = slot_rows.shape[1]
    rim_count = max(1, count // 8)
    source = jnp.concatenate([blocks, shared_blocks(blocks[:rim_count])], 0)
    picked = jnp.take(source, slot_rows.reshape(-1), axis=0).reshape(
        count, slot_count, value.shape[0], PB
    )
    tile_parts = tile_rows.reshape(count, PB, slot_count, PB)
    used = (lax.broadcasted_iota(jnp.int32, (count, slot_count), 1) < live_rows[:, None]).astype(
        jnp.float32
    )
    weights = scale_rows * used
    result = jnp.zeros((count, value.shape[0], PB), jnp.float32)
    for slot in range(slot_count):
        partial_rows = jnp.einsum(
            "bfc,brc->bfr",
            picked[:, slot],
            tile_parts[:, :, slot],
            preferred_element_type=jnp.float32,
        )
        result = result + weights[:, slot][:, None, None] * partial_rows
    return result.transpose(1, 0, 2).reshape(value.shape[0], 1, 1, count * PB)


def body(features, tiles, scales, slots, live, times):
    count = tiles.shape[2]
    tile_rows = tiles.reshape(count, PB, tiles.shape[4])
    scale_rows = scales.reshape(count, scales.shape[3])
    slot_rows = slots.reshape(count, slots.shape[3])
    live_rows = live.reshape(count)
    total = features.astype(jnp.float32)
    factor = jnp.ones(times.shape, jnp.float32)
    value = features
    for term in range(1, TERMS + 1):
        image = apply_operator(value, tile_rows, scale_rows, slot_rows, live_rows)
        factor = factor * -times / jnp.float32(term)
        total = total + factor[:, None, None, None] * image
        value = image.astype(jnp.bfloat16)
    return total.astype(jnp.bfloat16)


def solution(mesh):
    return jax.shard_map(
        body,
        mesh=mesh,
        in_specs=(
            P(None, "gx", "gy", "gz"),
            P("gx", "gy", "gz", None, None),
            P("gx", "gy", "gz", None),
            P("gx", "gy", "gz", None),
            P("gx", "gy", "gz"),
            P(),
        ),
        out_specs=P(None, "gx", "gy", "gz"),
        check_vma=False,
    )
```

profile of v0, /device:TPU:0, one launch (start us, length us, event | category | flops | bytes accessed | tf_op | source)
XLA Modules:
  0.0 181.4 jit_solution(16395035376558209992)
XLA Ops:
  0.0 1.6 reshape.173
  2.0 6.5 %all-gather = bf16[4,4,4096]{2,1,0:T(4,128)(2,1)S(1)} all-gather(bf16[1,4,4096]{2,1,0:T(4,128)(2,1)S(1)} %reshape.216), channel_id=1, replica_groups=mesh['gx'=2,'gy'=4,'gz'=4] {'gz'}, dimensions={0}, use_global_device_ids=true | all-gather | bytes 163840 | tf_op jit(solution)/shard_map/all_gather | solution.py:38
  8.5 3.8 %collective-permute-start = (bf16[1,1,16,4096]{3,2,1,0:T(8,128)(2,1)S(1)}, bf16[1,1,16,4096]{3,2,1,0:T(8,128)(2,1)S(1)}, u32[]{:S(2)}, u32[]{:S(2)}) collective-permute-start(bf16[1,1,16,4096]{3,2,1,0:T(8,128)(2,1)S(1)} %reshape.175), channel_id=1, source_target_pairs={{0,16},{1,17},{2,18},{3,19},{4,20},{5,21},{6,22},{7,23},{8,24},{9,... | collective-permute-start | bytes 393224 | tf_op jit(solution)/shard_map/ppermute | solution.py:18
  14.5 3.7 %reshape_reshape.5 = bf16[32,64,8,64]{3,2,1,0:T(8,128)(2,1)} reshape(bf16[1,1,32,64,512]{4,3,2,1,0:T(8,128)(2,1)S(1)} %copy-done.29) | data formatting | bytes 4194304 | tf_op jit(solution)/shard_map/reshape;reshape | solution.py:52
  18.1 23.5 %fusion.22 = (bf16[32,64,1,64]{3,2,1,0:T(2,128)(2,1)}, bf16[32,64,1,64]{3,2,1,0:T(2,128)(2,1)}, bf16[32,64,1,64]{3,2,1,0:T(2,128)(2,1)}, bf16[32,64,1,64]{3,2,1,...) fusion(bf16[32,64,8,64]{3,2,1,0:T(8,128)(2,1)} %reshape_reshape.5), kind=kLoop, calls=%fused_computation.116 | loop fusion | bytes 4194304 | tf_op jit(solution)/shard_map/slice | solution.py:62
  42.2 3.5 %collective-permute-start.2 = (bf16[3,1,16,4096]{3,2,1,0:T(8,128)(2,1)S(1)}, bf16[3,1,16,4096]{3,2,1,0:T(8,128)(2,1)S(1)}, u32[]{:S(2)}, u32[]{:S(2)}) collective-permute-start(bf16[3,1,16,4096]{3,2,1,0:T(8,128)(2,1)S(1)} %constant_dynamic-update-slice_fusion), channel_id=1, source_target_pairs={{0,4},{4,8},{8,12},{1,5},{5,9},{9,13},{2,6},{6,10},{10,14},{3,7},{... | collective-permute-start | bytes 1179656 | tf_op jit(solution)/shard_map/ppermute | solution.py:18
  48.2 6.1 %collective-permute-done.2 = bf16[3,1,16,4096]{3,2,1,0:T(8,128)(2,1)S(1)} collective-permute-done((bf16[3,1,16,4096]{3,2,1,0:T(8,128)(2,1)S(1)}, bf16[3,1,16,4096]{3,2,1,0:T(8,128)(2,1)S(1)}, u32[]{:S(2)}, u32[]{:S(2)}) %collective-permute-start.2) | collective-permute-done | bytes 393248 | tf_op jit(solution)/shard_map/ppermute | solution.py:18
  54.3 4.1 %collective-permute-done.3 = bf16[3,1,16,4096]{3,2,1,0:T(8,128)(2,1)S(1)} collective-permute-done((bf16[3,1,16,4096]{3,2,1,0:T(8,128)(2,1)S(1)}, bf16[3,1,16,4096]{3,2,1,0:T(8,128)(2,1)S(1)}, u32[]{:S(2)}, u32[]{:S(2)}) %collective-permute-start.3) | collective-permute-done | bytes 393248 | tf_op jit(solution)/shard_map/ppermute | solution.py:20
  58.7 1.8 %gather_fusion = bf16[256,4096]{1,0:T(8,128)(2,1)S(1)} fusion(bf16[176,4096]{1,0:T(8,128)(2,1)S(1)} %pad_maximum_fusion, s32[1024]{0:T(1024)S(1)} %pad_clamp_fusion), kind=kCustom, calls=%fused_computation.clone | custom fusion | bytes 4195328 | tf_op jit(solution)/shard_map/jit(_take)/gather | solution.py:49
  60.6 2.3 %broadcast_select_fusion.2 = bf16[256,4096]{1,0:T(8,128)(2,1)} fusion(bf16[256,4096]{1,0:T(8,128)(2,1)S(1)} %gather_fusion, pred[256]{0:T(512)(128)(4,1)} %compare_and_fusion), kind=kLoop, calls=%fused_computation.5 | loop fusion | flops 1048576 | bytes 4194560 | tf_op jit(solution)/shard_map/jit(_take)/select_n | solution.py:49
  62.9 7.0 %reshape.177 = bf16[32,8,64,64]{3,2,1,0:T(8,128)(2,1)} reshape(bf16[256,4096]{1,0:T(8,128)(2,1)} %broadcast_select_fusion.2) | data formatting | bytes 4194304 | tf_op jit(solution)/shard_map/reshape | solution.py:49
  69.9 1.6 convolution_multiply_fusion.23
  77.7 5.4 %all-gather.1 = bf16[4,4,4096]{2,1,0:T(4,128)(2,1)S(1)} all-gather(bf16[1,4,4096]{2,1,0:T(4,128)(2,1)S(1)} %reshape.218), channel_id=1, replica_groups=mesh['gx'=2,'gy'=4,'gz'=4] {'gz'}, dimensions={0}, use_global_device_ids=true | all-gather | bytes 163840 | tf_op jit(solution)/shard_map/all_gather | solution.py:38
  83.2 4.3 %collective-permute-start.4 = (bf16[1,1,16,4096]{3,2,1,0:T(8,128)(2,1)S(1)}, bf16[1,1,16,4096]{3,2,1,0:T(8,128)(2,1)S(1)}, u32[]{:S(2)}, u32[]{:S(2)}) collective-permute-start(bf16[1,1,16,4096]{3,2,1,0:T(8,128)(2,1)S(1)} %reshape.180), channel_id=1, source_target_pairs={{0,16},{1,17},{2,18},{3,19},{4,20},{5,21},{6,22},{7,23},{8,24},{9,... | collective-permute-start | bytes 393224 | tf_op jit(solution)/shard_map/ppermute | solution.py:18
  88.8 1.9 %collective-permute-done.4 = bf16[1,1,16,4096]{3,2,1,0:T(8,128)(2,1)S(1)} collective-permute-done((bf16[1,1,16,4096]{3,2,1,0:T(8,128)(2,1)S(1)}, bf16[1,1,16,4096]{3,2,1,0:T(8,128)(2,1)S(1)}, u32[]{:S(2)}, u32[]{:S(2)}) %collective-permute-start.4) | collective-permute-done | bytes 131104 | tf_op jit(solution)/shard_map/ppermute | solution.py:18
  90.8 4.1 %collective-permute-done.5 = bf16[1,1,16,4096]{3,2,1,0:T(8,128)(2,1)S(1)} collective-permute-done((bf16[1,1,16,4096]{3,2,1,0:T(8,128)(2,1)S(1)}, bf16[1,1,16,4096]{3,2,1,0:T(8,128)(2,1)S(1)}, u32[]{:S(2)}, u32[]{:S(2)}) %collective-permute-start.5) | collective-permute-done | bytes 131104 | tf_op jit(solution)/shard_map/ppermute | solution.py:20
  94.9 3.5 %collective-permute-start.6 = (bf16[3,1,16,4096]{3,2,1,0:T(8,128)(2,1)S(1)}, bf16[3,1,16,4096]{3,2,1,0:T(8,128)(2,1)S(1)}, u32[]{:S(2)}, u32[]{:S(2)}) collective-permute-start(bf16[3,1,16,4096]{3,2,1,0:T(8,128)(2,1)S(1)} %constant_dynamic-update-slice_fusion.3), channel_id=1, source_target_pairs={{0,4},{4,8},{8,12},{1,5},{5,9},{9,13},{2,6},{6,10},{10,14},{3,7},{... | collective-permute-start | bytes 1179656 | tf_op jit(solution)/shard_map/ppermute | solution.py:18
  100.3 5.8 %collective-permute-done.6 = bf16[3,1,16,4096]{3,2,1,0:T(8,128)(2,1)S(1)} collective-permute-done((bf16[3,1,16,4096]{3,2,1,0:T(8,128)(2,1)S(1)}, bf16[3,1,16,4096]{3,2,1,0:T(8,128)(2,1)S(1)}, u32[]{:S(2)}, u32[]{:S(2)}) %collective-permute-start.6) | collective-permute-done | bytes 393248 | tf_op jit(solution)/shard_map/ppermute | solution.py:18
  106.1 4.1 %collective-permute-done.7 = bf16[3,1,16,4096]{3,2,1,0:T(8,128)(2,1)S(1)} collective-permute-done((bf16[3,1,16,4096]{3,2,1,0:T(8,128)(2,1)S(1)}, bf16[3,1,16,4096]{3,2,1,0:T(8,128)(2,1)S(1)}, u32[]{:S(2)}, u32[]{:S(2)}) %collective-permute-start.7) | collective-permute-done | bytes 393248 | tf_op jit(solution)/shard_map/ppermute | solution.py:20
  110.5 1.8 %gather_fusion.1 = bf16[256,4096]{1,0:T(8,128)(2,1)S(1)} fusion(bf16[176,4096]{1,0:T(8,128)(2,1)S(1)} %pad_maximum_fusion.1, s32[1024]{0:T(1024)S(1)} %pad_clamp_fusion), kind=kCustom, calls=%fused_computation.1.clone | custom fusion | bytes 4195328 | tf_op jit(solution)/shard_map/jit(_take)/gather | solution.py:49
  112.3 2.3 %broadcast_select_fusion.1 = bf16[256,4096]{1,0:T(8,128)(2,1)} fusion(bf16[256,4096]{1,0:T(8,128)(2,1)S(1)} %gather_fusion.1, pred[256]{0:T(512)(128)(4,1)} %compare_and_fusion), kind=kLoop, calls=%fused_computation.4 | loop fusion | flops 1048576 | bytes 4194560 | tf_op jit(solution)/shard_map/jit(_take)/select_n | solution.py:49
  114.6 7.0 %reshape.182 = bf16[32,8,64,64]{3,2,1,0:T(8,128)(2,1)} reshape(bf16[256,4096]{1,0:T(8,128)(2,1)} %broadcast_select_fusion.1) | data formatting | bytes 4194304 | tf_op jit(solution)/shard_map/reshape | solution.py:49
  121.7 1.6 convolution_multiply_fusion.15
  129.3 5.4 %all-gather.2 = bf16[4,4,4096]{2,1,0:T(4,128)(2,1)S(1)} all-gather(bf16[1,4,4096]{2,1,0:T(4,128)(2,1)S(1)} %reshape.220), channel_id=1, replica_groups=mesh['gx'=2,'gy'=4,'gz'=4] {'gz'}, dimensions={0}, use_global_device_ids=true | all-gather | bytes 163840 | tf_op jit(solution)/shard_map/all_gather | solution.py:38
  137.6 2.1 %collective-permute-done.8 = bf16[1,1,16,4096]{3,2,1,0:T(8,128)(2,1)S(1)} collective-permute-done((bf16[1,1,16,4096]{3,2,1,0:T(8,128)(2,1)S(1)}, bf16[1,1,16,4096]{3,2,1,0:T(8,128)(2,1)S(1)}, u32[]{:S(2)}, u32[]{:S(2)}) %collective-permute-start.8) | collective-permute-done | bytes 131104 | tf_op jit(solution)/shard_map/ppermute | solution.py:18
  139.7 4.1 %collective-permute-done.9 = bf16[1,1,16,4096]{3,2,1,0:T(8,128)(2,1)S(1)} collective-permute-done((bf16[1,1,16,4096]{3,2,1,0:T(8,128)(2,1)S(1)}, bf16[1,1,16,4096]{3,2,1,0:T(8,128)(2,1)S(1)}, u32[]{:S(2)}, u32[]{:S(2)}) %collective-permute-start.9) | collective-permute-done | bytes 131104 | tf_op jit(solution)/shard_map/ppermute | solution.py:20
  143.8 4.2 %collective-permute-start.10 = (bf16[3,1,16,4096]{3,2,1,0:T(8,128)(2,1)S(1)}, bf16[3,1,16,4096]{3,2,1,0:T(8,128)(2,1)}, u32[]{:S(2)}, u32[]{:S(2)}) collective-permute-start(bf16[3,1,16,4096]{3,2,1,0:T(8,128)(2,1)S(1)} %constant_dynamic-update-slice_fusion.6), channel_id=1, source_target_pairs={{0,4},{4,8},{8,12},{1,5},{5,9},{9,13},{2,6},{6,10},{10,14},{3,7},{... | collective-permute-start | bytes 1179656 | tf_op jit(solution)/shard_map/ppermute | solution.py:18
  155.2 4.9 %collective-permute-done.11 = bf16[3,1,16,4096]{3,2,1,0:T(8,128)(2,1)} collective-permute-done((bf16[3,1,16,4096]{3,2,1,0:T(8,128)(2,1)S(1)}, bf16[3,1,16,4096]{3,2,1,0:T(8,128)(2,1)}, u32[]{:S(2)}, u32[]{:S(2)}) %collective-permute-start.11) | collective-permute-done | bytes 393248 | tf_op jit(solution)/shard_map/ppermute | solution.py:20
  161.5 1.8 %gather_fusion.2 = bf16[256,4096]{1,0:T(8,128)(2,1)S(1)} fusion(bf16[176,4096]{1,0:T(8,128)(2,1)S(1)} %pad_maximum_fusion.2, s32[1024]{0:T(1024)S(1)} %pad_clamp_fusion), kind=kCustom, calls=%fused_computation.2.clone | custom fusion | bytes 4195328 | tf_op jit(solution)/shard_map/jit(_take)/gather | solution.py:49
  163.3 2.3 %broadcast_select_fusion = bf16[256,4096]{1,0:T(8,128)(2,1)} fusion(bf16[256,4096]{1,0:T(8,128)(2,1)S(1)} %gather_fusion.2, pred[256]{0:T(512)(128)(4,1)} %compare_and_fusion), kind=kLoop, calls=%fused_computation.3 | loop fusion | flops 1048576 | bytes 4194560 | tf_op jit(solution)/shard_map/jit(_take)/select_n | solution.py:49
  165.6 7.0 %reshape.187 = bf16[32,8,64,64]{3,2,1,0:T(8,128)(2,1)} reshape(bf16[256,4096]{1,0:T(8,128)(2,1)} %broadcast_select_fusion) | data formatting | bytes 4194304 | tf_op jit(solution)/shard_map/reshape | solution.py:49
  172.7 1.6 convolution_multiply_fusion.7
  (182 shorter events, 39.5 us)
Async XLA Ops:
  0.0 14.5 %copy-start.29 = (bf16[1,1,32,64,512]{4,3,2,1,0:T(8,128)(2,1)S(1)}, bf16[1,1,32,64,512]{4,3,2,1,0:T(8,128)(2,1)}, u32[]{:S(2)}) copy-start(bf16[1,1,32,64,512]{4,3,2,1,0:T(8,128)(2,1)} %param.9) | copy-start | bytes 6291460
  8.5 33.7 %collective-permute-start = (bf16[1,1,16,4096]{3,2,1,0:T(8,128)(2,1)S(1)}, bf16[1,1,16,4096]{3,2,1,0:T(8,128)(2,1)S(1)}, u32[]{:S(2)}, u32[]{:S(2)}) collective-permute-start(bf16[1,1,16,4096]{3,2,1,0:T(8,128)(2,1)S(1)} %reshape.175), channel_id=1, source_target_pairs={{0,16},{1,17},{2,18},{3,19},{4,20},{5,21},{6,22},{7,23},{8,24},{9,... | collective-permute-start | bytes 393224 | tf_op jit(solution)/shard_map/ppermute | solution.py:18
  12.3 29.9 %collective-permute-start.1 = (bf16[1,1,16,4096]{3,2,1,0:T(8,128)(2,1)S(1)}, bf16[1,1,16,4096]{3,2,1,0:T(8,128)(2,1)S(1)}, u32[]{:S(2)}, u32[]{:S(2)}) collective-permute-start(bf16[1,1,16,4096]{3,2,1,0:T(8,128)(2,1)S(1)} %reshape.175), channel_id=1, source_target_pairs={{16,0},{17,1},{18,2},{19,3},{20,4},{21,5},{22,6},{23,7},{24,8},{25... | collective-permute-start | bytes 393224 | tf_op jit(solution)/shard_map/ppermute | solution.py:20
  18.1 23.5 %copy-start.48 = (f32[1,1,32,8]{2,3,1,0:T(8,128)S(1)}, f32[1,1,32,8]{2,3,1,0:T(8,128)}, u32[]{:S(2)}) copy-start(f32[1,1,32,8]{2,3,1,0:T(8,128)} %param.10) | copy-start | bytes 3076
  18.1 23.5 %copy-start.52 = (s32[1,1,32]{2,1,0:T(1,128)S(1)}, s32[1,1,32]{2,1,0:T(1,128)}, u32[]{:S(2)}) copy-start(s32[1,1,32]{2,1,0:T(1,128)} %param.12) | copy-start | bytes 388
  42.2 12.1 %collective-permute-start.2 = (bf16[3,1,16,4096]{3,2,1,0:T(8,128)(2,1)S(1)}, bf16[3,1,16,4096]{3,2,1,0:T(8,128)(2,1)S(1)}, u32[]{:S(2)}, u32[]{:S(2)}) collective-permute-start(bf16[3,1,16,4096]{3,2,1,0:T(8,128)(2,1)S(1)} %constant_dynamic-update-slice_fusion), channel_id=1, source_target_pairs={{0,4},{4,8},{8,12},{1,5},{5,9},{9,13},{2,6},{6,10},{10,14},{3,7},{... | collective-permute-start | bytes 1179656 | tf_op jit(solution)/shard_map/ppermute | solution.py:18
  45.7 12.7 %collective-permute-start.3 = (bf16[3,1,16,4096]{3,2,1,0:T(8,128)(2,1)S(1)}, bf16[3,1,16,4096]{3,2,1,0:T(8,128)(2,1)S(1)}, u32[]{:S(2)}, u32[]{:S(2)}) collective-permute-start(bf16[3,1,16,4096]{3,2,1,0:T(8,128)(2,1)S(1)} %constant_dynamic-update-slice_fusion), channel_id=1, source_target_pairs={{4,0},{8,4},{12,8},{5,1},{9,5},{13,9},{6,2},{10,6},{14,10},{7,3},{... | collective-permute-start | bytes 1179656 | tf_op jit(solution)/shard_map/ppermute | solution.py:20
  62.8 7.1 %copy-start.3 = (bf16[32,64,1,64]{3,2,1,0:T(2,128)(2,1)S(1)}, bf16[32,64,1,64]{3,2,1,0:T(2,128)(2,1)}, u32[]{:S(2)}) copy-start(bf16[32,64,1,64]{3,2,1,0:T(2,128)(2,1)} %get-tuple-element.13) | copy-start | bytes 786436
  62.8 8.7 %copy-start.24 = (bf16[32,64,1,64]{3,2,1,0:T(2,128)(2,1)S(1)}, bf16[32,64,1,64]{3,2,1,0:T(2,128)(2,1)}, u32[]{:S(2)}) copy-start(bf16[32,64,1,64]{3,2,1,0:T(2,128)(2,1)} %get-tuple-element.12) | copy-start | bytes 786436
  62.9 8.7 %copy-start.42 = (f32[32]{0:T(128)S(1)}, f32[32]{0:T(128)}, u32[]{:S(2)}) copy-start(f32[32]{0:T(128)} %get-tuple-element.20) | copy-start | bytes 388
  69.9 3.2 %copy-start.21 = (bf16[32,64,1,64]{3,2,1,0:T(2,128)(2,1)S(1)}, bf16[32,64,1,64]{3,2,1,0:T(2,128)(2,1)}, u32[]{:S(2)}) copy-start(bf16[32,64,1,64]{3,2,1,0:T(2,128)(2,1)} %get-tuple-element.11) | copy-start | bytes 786436
  69.9 3.3 %copy-start.39 = (f32[32]{0:T(128)S(1)}, f32[32]{0:T(128)}, u32[]{:S(2)}) copy-start(f32[32]{0:T(128)} %get-tuple-element.19) | copy-start | bytes 388
  83.2 7.5 %collective-permute-start.4 = (bf16[1,1,16,4096]{3,2,1,0:T(8,128)(2,1)S(1)}, bf16[1,1,16,4096]{3,2,1,0:T(8,128)(2,1)S(1)}, u32[]{:S(2)}, u32[]{:S(2)}) collective-permute-start(bf16[1,1,16,4096]{3,2,1,0:T(8,128)(2,1)S(1)} %reshape.180), channel_id=1, source_target_pairs={{0,16},{1,17},{2,18},{3,19},{4,20},{5,21},{6,22},{7,23},{8,24},{9,... | collective-permute-start | bytes 393224 | tf_op jit(solution)/shard_map/ppermute | solution.py:18
  87.5 7.4 %collective-permute-start.5 = (bf16[1,1,16,4096]{3,2,1,0:T(8,128)(2,1)S(1)}, bf16[1,1,16,4096]{3,2,1,0:T(8,128)(2,1)S(1)}, u32[]{:S(2)}, u32[]{:S(2)}) collective-permute-start(bf16[1,1,16,4096]{3,2,1,0:T(8,128)(2,1)S(1)} %reshape.180), channel_id=1, source_target_pairs={{16,0},{17,1},{18,2},{19,3},{20,4},{21,5},{22,6},{23,7},{24,8},{25... | collective-permute-start | bytes 393224 | tf_op jit(solution)/shard_map/ppermute | solution.py:20
  94.9 11.2 %collective-permute-start.6 = (bf16[3,1,16,4096]{3,2,1,0:T(8,128)(2,1)S(1)}, bf16[3,1,16,4096]{3,2,1,0:T(8,128)(2,1)S(1)}, u32[]{:S(2)}, u32[]{:S(2)}) collective-permute-start(bf16[3,1,16,4096]{3,2,1,0:T(8,128)(2,1)S(1)} %constant_dynamic-update-slice_fusion.3), channel_id=1, source_target_pairs={{0,4},{4,8},{8,12},{1,5},{5,9},{9,13},{2,6},{6,10},{10,14},{3,7},{... | collective-permute-start | bytes 1179656 | tf_op jit(solution)/shard_map/ppermute | solution.py:18
  98.4 11.9 %collective-permute-start.7 = (bf16[3,1,16,4096]{3,2,1,0:T(8,128)(2,1)S(1)}, bf16[3,1,16,4096]{3,2,1,0:T(8,128)(2,1)S(1)}, u32[]{:S(2)}, u32[]{:S(2)}) collective-permute-start(bf16[3,1,16,4096]{3,2,1,0:T(8,128)(2,1)S(1)} %constant_dynamic-update-slice_fusion.3), channel_id=1, source_target_pairs={{4,0},{8,4},{12,8},{5,1},{9,5},{13,9},{6,2},{10,6},{14,10},{7,3},{... | collective-permute-start | bytes 1179656 | tf_op jit(solution)/shard_map/ppermute | solution.py:20
  114.6 7.1 %copy-start.4 = (bf16[32,64,1,64]{3,2,1,0:T(2,128)(2,1)S(1)}, bf16[32,64,1,64]{3,2,1,0:T(2,128)(2,1)}, u32[]{:S(2)}) copy-start(bf16[32,64,1,64]{3,2,1,0:T(2,128)(2,1)} %get-tuple-element.13) | copy-start | bytes 786436
  114.6 8.7 %copy-start.25 = (bf16[32,64,1,64]{3,2,1,0:T(2,128)(2,1)S(1)}, bf16[32,64,1,64]{3,2,1,0:T(2,128)(2,1)}, u32[]{:S(2)}) copy-start(bf16[32,64,1,64]{3,2,1,0:T(2,128)(2,1)} %get-tuple-element.12) | copy-start | bytes 786436
  114.6 8.7 %copy-start.43 = (f32[32]{0:T(128)S(1)}, f32[32]{0:T(128)}, u32[]{:S(2)}) copy-start(f32[32]{0:T(128)} %get-tuple-element.20) | copy-start | bytes 388
  121.7 3.2 %copy-start.22 = (bf16[32,64,1,64]{3,2,1,0:T(2,128)(2,1)S(1)}, bf16[32,64,1,64]{3,2,1,0:T(2,128)(2,1)}, u32[]{:S(2)}) copy-start(bf16[32,64,1,64]{3,2,1,0:T(2,128)(2,1)} %get-tuple-element.11) | copy-start | bytes 786436
  121.7 3.3 %copy-start.40 = (f32[32]{0:T(128)S(1)}, f32[32]{0:T(128)}, u32[]{:S(2)}) copy-start(f32[32]{0:T(128)} %get-tuple-element.19) | copy-start | bytes 388
  128.0 21.5 %copy-start.53 = (f32[64]{0:T(128)S(1)}, f32[64]{0:T(128)}, u32[]{:S(2)}) copy-start(f32[64]{0:T(128)} %param.13) | copy-start | bytes 772
  128.0 22.1 %copy-start.27 = (f32[32,64,64]{2,1,0:T(8,128)S(1)}, f32[32,64,64]{2,1,0:T(8,128)}, u32[]{:S(2)}) copy-start(f32[32,64,64]{2,1,0:T(8,128)} %get-tuple-element.26) | copy-start | bytes 1572868
  134.8 4.8 %collective-permute-start.8 = (bf16[1,1,16,4096]{3,2,1,0:T(8,128)(2,1)S(1)}, bf16[1,1,16,4096]{3,2,1,0:T(8,128)(2,1)S(1)}, u32[]{:S(2)}, u32[]{:S(2)}) collective-permute-start(bf16[1,1,16,4096]{3,2,1,0:T(8,128)(2,1)S(1)} %reshape.185), channel_id=1, source_target_pairs={{0,16},{1,17},{2,18},{3,19},{4,20},{5,21},{6,22},{7,23},{8,24},{9,... | collective-permute-start | bytes 393224 | tf_op jit(solution)/shard_map/ppermute | solution.py:18
  136.3 7.5 %collective-permute-start.9 = (bf16[1,1,16,4096]{3,2,1,0:T(8,128)(2,1)S(1)}, bf16[1,1,16,4096]{3,2,1,0:T(8,128)(2,1)S(1)}, u32[]{:S(2)}, u32[]{:S(2)}) collective-permute-start(bf16[1,1,16,4096]{3,2,1,0:T(8,128)(2,1)S(1)} %reshape.185), channel_id=1, source_target_pairs={{16,0},{17,1},{18,2},{19,3},{20,4},{21,5},{22,6},{23,7},{24,8},{25... | collective-permute-start | bytes 393224 | tf_op jit(solution)/shard_map/ppermute | solution.py:20
  143.8 11.4 %collective-permute-start.10 = (bf16[3,1,16,4096]{3,2,1,0:T(8,128)(2,1)S(1)}, bf16[3,1,16,4096]{3,2,1,0:T(8,128)(2,1)}, u32[]{:S(2)}, u32[]{:S(2)}) collective-permute-start(bf16[3,1,16,4096]{3,2,1,0:T(8,128)(2,1)S(1)} %constant_dynamic-update-slice_fusion.6), channel_id=1, source_target_pairs={{0,4},{4,8},{8,12},{1,5},{5,9},{9,13},{2,6},{6,10},{10,14},{3,7},{... | collective-permute-start | bytes 1179656 | tf_op jit(solution)/shard_map/ppermute | solution.py:18
  148.0 12.1 %collective-permute-start.11 = (bf16[3,1,16,4096]{3,2,1,0:T(8,128)(2,1)S(1)}, bf16[3,1,16,4096]{3,2,1,0:T(8,128)(2,1)}, u32[]{:S(2)}, u32[]{:S(2)}) collective-permute-start(bf16[3,1,16,4096]{3,2,1,0:T(8,128)(2,1)S(1)} %constant_dynamic-update-slice_fusion.6), channel_id=1, source_target_pairs={{4,0},{8,4},{12,8},{5,1},{9,5},{13,9},{6,2},{10,6},{14,10},{7,3},{... | collective-permute-start | bytes 1179656 | tf_op jit(solution)/shard_map/ppermute | solution.py:20
  165.6 7.1 %copy-start.5 = (bf16[32,64,1,64]{3,2,1,0:T(2,128)(2,1)S(1)}, bf16[32,64,1,64]{3,2,1,0:T(2,128)(2,1)}, u32[]{:S(2)}) copy-start(bf16[32,64,1,64]{3,2,1,0:T(2,128)(2,1)} %get-tuple-element.13) | copy-start | bytes 786436
  165.6 8.7 %copy-start.26 = (bf16[32,64,1,64]{3,2,1,0:T(2,128)(2,1)S(1)}, bf16[32,64,1,64]{3,2,1,0:T(2,128)(2,1)}, u32[]{:S(2)}) copy-start(bf16[32,64,1,64]{3,2,1,0:T(2,128)(2,1)} %get-tuple-element.12) | copy-start | bytes 786436
  165.6 8.7 %copy-start.44 = (f32[32]{0:T(128)S(1)}, f32[32]{0:T(128)}, u32[]{:S(2)}) copy-start(f32[32]{0:T(128)} %get-tuple-element.20) | copy-start | bytes 388
  172.7 3.2 %copy-start.23 = (bf16[32,64,1,64]{3,2,1,0:T(2,128)(2,1)S(1)}, bf16[32,64,1,64]{3,2,1,0:T(2,128)(2,1)}, u32[]{:S(2)}) copy-start(bf16[32,64,1,64]{3,2,1,0:T(2,128)(2,1)} %get-tuple-element.11) | copy-start | bytes 786436
  172.7 3.3 %copy-start.41 = (f32[32]{0:T(128)S(1)}, f32[32]{0:T(128)}, u32[]{:S(2)}) copy-start(f32[32]{0:T(128)} %get-tuple-element.19) | copy-start | bytes 388
  (34 other events, 54.7 us)
where the time goes:
time: 182 us; the launch traced here: 181 us
  local copies, waits for them, and re-layouts  68.4 us (38%)
  waiting for transfers between devices  37.3 us (20%)
  starting transfers between devices  28.9 us (16%)
  matrix products  17.7 us (10%)
  blocking collectives  17.3 us (10%)
  other arithmetic  10.8 us (6%)
    slice x1, local copies, waits for them, and re-layouts, apply_operator(): tile_parts[:, :, slot]  23.5 us
    ppermute x6, waiting for transfers between devices, with_halo(): lax.ppermute(head, axis, [((i + 1) % count, i) for i in range(ends)])  21.4 us
    reshape x3, local copies, waits for them, and re-layouts, apply_operator(): jnp.take(source, slot_rows.reshape(-1), axis=0)  21.1 us
    ppermute x6, starting transfers between devices, with_halo(): lax.ppermute(tail, axis, [(i, (i + 1) % count) for i in range(ends)])  20.8 us
    dot_general x24, matrix products, apply_operator(): jnp.einsum('bfc,brc->bfr', picked[:, slot], tile_parts[:, :, slot], prefe...  17.7 us
    all_gather x3, blocking collectives, shared_blocks(): panel = lax.all_gather(rim_rows, 'gz', axis=0, tiled=True)  17.3 us
    ppermute x6, waiting for transfers between devices, with_halo(): lax.ppermute(tail, axis, [(i, (i + 1) % count) for i in range(ends)])  15.9 us
    ppermute x6, starting transfers between devices, with_halo(): lax.ppermute(head, axis, [((i + 1) % count, i) for i in range(ends)])  8.14 us
  transfers between devices with their start and end apart: 12, of which 9 were waited for; matrix products, arithmetic and copies ran while one was open for 20% of the time, Pallas kernels for 0%

commit v1 on v0

--- a/solution.py
+++ b/solution.py
@@ -35,7 +35,34 @@
 
 def shared_blocks(rim_rows):
     width = rim_rows.shape[1]
-    panel = lax.all_gather(rim_rows, "gz", axis=0, tiled=True)
+    all_blocks = []
+    outcome_arr, wide_out, local_out = (
+        jax.lax.axis_size("gz"),
+        jax.lax.axis_index("gz"),
+        rim_rows.shape[0],
+    )
+    for d, w in enumerate(rim_rows.shape):
+        all_blocks.append(w * outcome_arr if d == 0 else w)
+    panel = lax.dynamic_update_slice_in_dim(
+        jnp.zeros(all_blocks, rim_rows.dtype), rim_rows, wide_out * local_out, axis=0
+    )
+    y2 = y_new = rim_rows
+    for rr in range(1, outcome_arr // 2 + 1):
+        seen = []
+        for d in range(outcome_arr):
+            seen.append((d, (d + 1) % outcome_arr))
+        y2 = jax.lax.ppermute(y2, axis_name="gz", perm=seen)
+        panel = lax.dynamic_update_slice_in_dim(
+            panel, y2, (wide_out - rr) % outcome_arr * local_out, axis=0
+        )
+        if 2 * rr < outcome_arr:
+            row_list = []
+            for d in range(outcome_arr):
+                row_list.append((d, (d - 1) % outcome_arr))
+            y_new = jax.lax.ppermute(y_new, axis_name="gz", perm=row_list)
+            panel = lax.dynamic_update_slice_in_dim(
+                panel, y_new, (wide_out + rr) % outcome_arr * local_out, axis=0
+            )
     grid = with_halo(panel.reshape(1, 1, panel.shape[0], width), (("gx", 0), ("gy", 1)), 1)
     return grid.reshape(-1, width)
 

time: 182 us -> 189 us (1.038)
  blocking collectives: 17.3 us -> 0 us
  waiting for transfers between devices: 37.3 us -> 47.9 us
  local copies, waits for them, and re-layouts: 68.4 us -> 75.7 us
  starting transfers between devices: 28.9 us -> 33.7 us
    all_gather x3 -> x0, blocking collectives: 17.3 us -> none  [shared_blocks(): panel = lax.all_gather(rim_rows, 'gz', axis=0, tiled=True)]
    ppermute x0 -> x9, waiting for transfers between devices: none -> 12.3 us  [the longest x6 12.3 us: shared_blocks(): y2 = jax.lax.ppermute(y2, axis_name='gz', perm=seen)]
    unnamed x118 -> x111, local copies, waits for them, and re-layouts: 5 us -> 11.8 us
    ppermute x0 -> x9, starting transfers between devices: none -> 6.74 us  [the longest x3 5.45 us: shared_blocks(): y_new = jax.lax.ppermute(y_new, axis_name='gz', perm=row_list)]
    ppermute x6, waiting for transfers between devices: 15.9 us -> 10.5 us  [with_halo(): lax.ppermute(tail, axis, [(i, (i + 1) % count) for i in range(ends)])]
    ppermute x6, waiting for transfers between devices: 21.4 us -> 25.1 us  [with_halo(): lax.ppermute(head, axis, [((i + 1) % count, i) for i in range(ends)])]
    ppermute x6, starting transfers between devices: 20.8 us -> 18.8 us  [with_halo(): lax.ppermute(tail, axis, [(i, (i + 1) % count) for i in range(ends)])]
  transfers between devices with their start and end apart: 12 -> 21, of which waited for: 9 -> 16; matrix products, arithmetic and copies ran while one was open for 20% -> 19% of each run, Pallas kernels for 0% -> 0%
where the time goes in v1:
time: 189 us; the launch traced here: 188 us
  local copies, waits for them, and re-layouts  75.7 us (40%)
  waiting for transfers between devices  47.9 us (25%)
  starting transfers between devices  33.7 us (18%)
  matrix products  17.6 us (9%)
  other arithmetic  11.6 us (6%)
    ppermute x6, waiting for transfers between devices, with_halo(): lax.ppermute(head, axis, [((i + 1) % count, i) for i in range(ends)])  25.1 us
    slice x1, local copies, waits for them, and re-layouts, apply_operator(): tile_parts[:, :, slot]  23 us
    reshape x3, local copies, waits for them, and re-layouts, apply_operator(): jnp.take(source, slot_rows.reshape(-1), axis=0)  21.2 us
    ppermute x6, starting transfers between devices, with_halo(): lax.ppermute(tail, axis, [(i, (i + 1) % count) for i in range(ends)])  18.8 us
    dot_general x24, matrix products, apply_operator(): jnp.einsum('bfc,brc->bfr', picked[:, slot], tile_parts[:, :, slot], prefe...  17.6 us
    ppermute x6, waiting for transfers between devices, shared_blocks(): y2 = jax.lax.ppermute(y2, axis_name='gz', perm=seen)  12.3 us
    unnamed x111, local copies, waits for them, and re-layouts  11.8 us
    ppermute x6, waiting for transfers between devices, with_halo(): lax.ppermute(tail, axis, [(i, (i + 1) % count) for i in range(ends)])  10.5 us
  transfers between devices with their start and end apart: 21, of which 16 were waited for; matrix products, arithmetic and copies ran while one was open for 19% of the time, Pallas kernels for 0%

profile of v1, /device:TPU:0, one launch (start us, length us, event | category | flops | bytes accessed | tf_op | source)
XLA Modules:
  0.0 187.6 jit_solution(2849544399254748570)
XLA Ops:
  0.0 1.6 reshape.220
  2.5 2.0 %collective-permute-start.1 = (bf16[4,4096]{1,0:T(4,128)(2,1)S(1)}, bf16[4,4096]{1,0:T(4,128)(2,1)S(1)}, u32[]{:S(2)}, u32[]{:S(2)}) collective-permute-start(bf16[4,4096]{1,0:T(4,128)(2,1)S(1)} %slice.172), channel_id=1, source_target_pairs={{0,3},{1,0},{2,1},{3,2},{4,7},{5,4},{6,5},{7,6},{8,11},{9,8},{10,9... | collective-permute-start | bytes 98312 | tf_op jit(solution)/shard_map/ppermute | solution.py:62
  4.6 3.6 %reshape_reshape.5 = bf16[32,64,8,64]{3,2,1,0:T(8,128)(2,1)} reshape(bf16[1,1,32,64,512]{4,3,2,1,0:T(8,128)(2,1)S(1)} %copy-done.29) | data formatting | bytes 4194304 | tf_op jit(solution)/shard_map/reshape;reshape | solution.py:79
  8.2 23.0 %fusion.22 = (bf16[32,64,1,64]{3,2,1,0:T(2,128)(2,1)}, bf16[32,64,1,64]{3,2,1,0:T(2,128)(2,1)}, bf16[32,64,1,64]{3,2,1,0:T(2,128)(2,1)}, bf16[32,64,1,64]{3,2,1,...) fusion(bf16[32,64,8,64]{3,2,1,0:T(8,128)(2,1)} %reshape_reshape.5), kind=kLoop, calls=%fused_computation.122 | loop fusion | bytes 4194304 | tf_op jit(solution)/shard_map/slice | solution.py:89
  32.3 2.6 %collective-permute-done.2 = bf16[4,4096]{1,0:T(4,128)(2,1)S(1)} collective-permute-done((bf16[4,4096]{1,0:T(4,128)(2,1)S(1)}, bf16[4,4096]{1,0:T(4,128)(2,1)S(1)}, u32[]{:S(2)}, u32[]{:S(2)}) %collective-permute-start.2) | collective-permute-done | bytes 32800 | tf_op jit(solution)/shard_map/ppermute | solution.py:54
  35.0 4.2 %collective-permute-start.3 = (bf16[1,1,16,4096]{3,2,1,0:T(8,128)(2,1)S(1)}, bf16[1,1,16,4096]{3,2,1,0:T(8,128)(2,1)S(1)}, u32[]{:S(2)}, u32[]{:S(2)}) collective-permute-start(bf16[1,1,16,4096]{3,2,1,0:T(8,128)(2,1)S(1)} %bitcast_dynamic-update-slice_fusion.6), channel_id=1, source_target_pairs={{0,16},{1,17},{2,18},{3,19},{4,20},{5,21},{6,22},{7,23},{8,24},{9,... | collective-permute-start | bytes 393224 | tf_op jit(solution)/shard_map/ppermute | solution.py:18
  41.7 4.4 %collective-permute-done.4 = bf16[1,1,16,4096]{3,2,1,0:T(8,128)(2,1)S(1)} collective-permute-done((bf16[1,1,16,4096]{3,2,1,0:T(8,128)(2,1)S(1)}, bf16[1,1,16,4096]{3,2,1,0:T(8,128)(2,1)S(1)}, u32[]{:S(2)}, u32[]{:S(2)}) %collective-permute-start.4) | collective-permute-done | bytes 131104 | tf_op jit(solution)/shard_map/ppermute | solution.py:20
  46.1 3.5 %collective-permute-start.5 = (bf16[3,1,16,4096]{3,2,1,0:T(8,128)(2,1)S(1)}, bf16[3,1,16,4096]{3,2,1,0:T(8,128)(2,1)S(1)}, u32[]{:S(2)}, u32[]{:S(2)}) collective-permute-start(bf16[3,1,16,4096]{3,2,1,0:T(8,128)(2,1)S(1)} %pad_maximum_fusion.6), channel_id=1, source_target_pairs={{0,4},{4,8},{8,12},{1,5},{5,9},{9,13},{2,6},{6,10},{10,14},{3,7},{... | collective-permute-start | bytes 1179656 | tf_op jit(solution)/shard_map/ppermute | solution.py:18
  52.1 3.9 %collective-permute-done.5 = bf16[3,1,16,4096]{3,2,1,0:T(8,128)(2,1)S(1)} collective-permute-done((bf16[3,1,16,4096]{3,2,1,0:T(8,128)(2,1)S(1)}, bf16[3,1,16,4096]{3,2,1,0:T(8,128)(2,1)S(1)}, u32[]{:S(2)}, u32[]{:S(2)}) %collective-permute-start.5) | collective-permute-done | bytes 393248 | tf_op jit(solution)/shard_map/ppermute | solution.py:18
  56.0 4.1 %collective-permute-done.6 = bf16[3,1,16,4096]{3,2,1,0:T(8,128)(2,1)S(1)} collective-permute-done((bf16[3,1,16,4096]{3,2,1,0:T(8,128)(2,1)S(1)}, bf16[3,1,16,4096]{3,2,1,0:T(8,128)(2,1)S(1)}, u32[]{:S(2)}, u32[]{:S(2)}) %collective-permute-start.6) | collective-permute-done | bytes 393248 | tf_op jit(solution)/shard_map/ppermute | solution.py:20
  60.4 1.8 gather_fusion
  62.3 2.3 %broadcast_select_fusion.2 = bf16[256,4096]{1,0:T(8,128)(2,1)} fusion(bf16[256,4096]{1,0:T(8,128)(2,1)S(1)} %gather_fusion, pred[256]{0:T(512)(128)(4,1)} %compare_and_fusion), kind=kLoop, calls=%fused_computation.5 | loop fusion | flops 1048576 | bytes 4194560 | tf_op jit(solution)/shard_map/jit(_take)/select_n | solution.py:76
  64.5 7.0 %reshape.228 = bf16[32,8,64,64]{3,2,1,0:T(8,128)(2,1)} reshape(bf16[256,4096]{1,0:T(8,128)(2,1)} %broadcast_select_fusion.2) | data formatting | bytes 4194304 | tf_op jit(solution)/shard_map/reshape | solution.py:76
  81.1 1.7 collective-permute-start.8
  84.5 3.3 %collective-permute-done.9 = bf16[4,4096]{1,0:T(4,128)(2,1)S(1)} collective-permute-done((bf16[4,4096]{1,0:T(4,128)(2,1)S(1)}, bf16[4,4096]{1,0:T(4,128)(2,1)S(1)}, u32[]{:S(2)}, u32[]{:S(2)}) %collective-permute-start.9) | collective-permute-done | bytes 32800 | tf_op jit(solution)/shard_map/ppermute | solution.py:54
  87.8 1.8 collective-permute-start.10
  92.1 4.4 %collective-permute-done.11 = bf16[1,1,16,4096]{3,2,1,0:T(8,128)(2,1)S(1)} collective-permute-done((bf16[1,1,16,4096]{3,2,1,0:T(8,128)(2,1)S(1)}, bf16[1,1,16,4096]{3,2,1,0:T(8,128)(2,1)S(1)}, u32[]{:S(2)}, u32[]{:S(2)}) %collective-permute-start.11) | collective-permute-done | bytes 131104 | tf_op jit(solution)/shard_map/ppermute | solution.py:20
  96.5 3.5 %collective-permute-start.12 = (bf16[3,1,16,4096]{3,2,1,0:T(8,128)(2,1)S(1)}, bf16[3,1,16,4096]{3,2,1,0:T(8,128)(2,1)S(1)}, u32[]{:S(2)}, u32[]{:S(2)}) collective-permute-start(bf16[3,1,16,4096]{3,2,1,0:T(8,128)(2,1)S(1)} %pad_maximum_fusion.7), channel_id=1, source_target_pairs={{0,4},{4,8},{8,12},{1,5},{5,9},{9,13},{2,6},{6,10},{10,14},{3,7},{... | collective-permute-start | bytes 1179656 | tf_op jit(solution)/shard_map/ppermute | solution.py:18
  101.9 3.5 %collective-permute-done.12 = bf16[3,1,16,4096]{3,2,1,0:T(8,128)(2,1)S(1)} collective-permute-done((bf16[3,1,16,4096]{3,2,1,0:T(8,128)(2,1)S(1)}, bf16[3,1,16,4096]{3,2,1,0:T(8,128)(2,1)S(1)}, u32[]{:S(2)}, u32[]{:S(2)}) %collective-permute-start.12) | collective-permute-done | bytes 393248 | tf_op jit(solution)/shard_map/ppermute | solution.py:18
  105.4 4.3 %collective-permute-done.13 = bf16[3,1,16,4096]{3,2,1,0:T(8,128)(2,1)S(1)} collective-permute-done((bf16[3,1,16,4096]{3,2,1,0:T(8,128)(2,1)S(1)}, bf16[3,1,16,4096]{3,2,1,0:T(8,128)(2,1)S(1)}, u32[]{:S(2)}, u32[]{:S(2)}) %collective-permute-start.13) | collective-permute-done | bytes 393248 | tf_op jit(solution)/shard_map/ppermute | solution.py:20
  109.9 1.8 gather_fusion.1
  111.8 2.3 %broadcast_select_fusion.1 = bf16[256,4096]{1,0:T(8,128)(2,1)} fusion(bf16[256,4096]{1,0:T(8,128)(2,1)S(1)} %gather_fusion.1, pred[256]{0:T(512)(128)(4,1)} %compare_and_fusion), kind=kLoop, calls=%fused_computation.4 | loop fusion | flops 1048576 | bytes 4194560 | tf_op jit(solution)/shard_map/jit(_take)/select_n | solution.py:76
  114.0 7.1 %reshape.236 = bf16[32,8,64,64]{3,2,1,0:T(8,128)(2,1)} reshape(bf16[256,4096]{1,0:T(8,128)(2,1)} %broadcast_select_fusion.1) | data formatting | bytes 4194304 | tf_op jit(solution)/shard_map/reshape | solution.py:76
  132.0 1.7 collective-permute-start.15
  135.4 3.3 %collective-permute-done.16 = bf16[4,4096]{1,0:T(4,128)(2,1)S(1)} collective-permute-done((bf16[4,4096]{1,0:T(4,128)(2,1)S(1)}, bf16[4,4096]{1,0:T(4,128)(2,1)S(1)}, u32[]{:S(2)}, u32[]{:S(2)}) %collective-permute-start.16) | collective-permute-done | bytes 32800 | tf_op jit(solution)/shard_map/ppermute | solution.py:54
  138.7 1.7 collective-permute-start.17
  142.9 4.4 %collective-permute-done.18 = bf16[1,1,16,4096]{3,2,1,0:T(8,128)(2,1)S(1)} collective-permute-done((bf16[1,1,16,4096]{3,2,1,0:T(8,128)(2,1)S(1)}, bf16[1,1,16,4096]{3,2,1,0:T(8,128)(2,1)S(1)}, u32[]{:S(2)}, u32[]{:S(2)}) %collective-permute-start.18) | collective-permute-done | bytes 131104 | tf_op jit(solution)/shard_map/ppermute | solution.py:20
  148.0 4.2 %collective-permute-start.19 = (bf16[3,1,16,4096]{3,2,1,0:T(8,128)(2,1)}, bf16[3,1,16,4096]{3,2,1,0:T(8,128)(2,1)}, u32[]{:S(2)}, u32[]{:S(2)}) collective-permute-start(bf16[3,1,16,4096]{3,2,1,0:T(8,128)(2,1)} %pad_maximum_fusion.8), channel_id=1, source_target_pairs={{0,4},{4,8},{8,12},{1,5},{5,9},{9,13},{2,6},{6,10},{10,14},{3,7},{... | collective-permute-start | bytes 1179656 | tf_op jit(solution)/shard_map/ppermute | solution.py:18
  159.4 3.6 %collective-permute-done.20 = bf16[3,1,16,4096]{3,2,1,0:T(8,128)(2,1)} collective-permute-done((bf16[3,1,16,4096]{3,2,1,0:T(8,128)(2,1)}, bf16[3,1,16,4096]{3,2,1,0:T(8,128)(2,1)}, u32[]{:S(2)}, u32[]{:S(2)}) %collective-permute-start.20) | collective-permute-done | bytes 393248 | tf_op jit(solution)/shard_map/ppermute | solution.py:20
  164.4 1.8 gather_fusion.2
  166.3 2.3 %broadcast_select_fusion = bf16[256,4096]{1,0:T(8,128)(2,1)} fusion(bf16[256,4096]{1,0:T(8,128)(2,1)S(1)} %gather_fusion.2, pred[256]{0:T(512)(128)(4,1)} %compare_and_fusion), kind=kLoop, calls=%fused_computation.3 | loop fusion | flops 1048576 | bytes 4194560 | tf_op jit(solution)/shard_map/jit(_take)/select_n | solution.py:76
  168.6 7.1 %reshape.244 = bf16[32,8,64,64]{3,2,1,0:T(8,128)(2,1)} reshape(bf16[256,4096]{1,0:T(8,128)(2,1)} %broadcast_select_fusion) | data formatting | bytes 4194304 | tf_op jit(solution)/shard_map/reshape | solution.py:76
  (208 shorter events, 58.9 us)
Async XLA Ops:
  2.0 29.6 %collective-permute-start = (bf16[4,4096]{1,0:T(4,128)(2,1)S(1)}, bf16[4,4096]{1,0:T(4,128)(2,1)S(1)}, u32[]{:S(2)}, u32[]{:S(2)}) collective-permute-start(bf16[4,4096]{1,0:T(4,128)(2,1)S(1)} %slice.172), channel_id=1, source_target_pairs={{0,1},{1,2},{2,3},{3,0},{4,5},{5,6},{6,7},{7,4},{8,9},{9,10},{10,1... | collective-permute-start | bytes 98312 | tf_op jit(solution)/shard_map/ppermute | solution.py:54
  2.5 29.8 %collective-permute-start.1 = (bf16[4,4096]{1,0:T(4,128)(2,1)S(1)}, bf16[4,4096]{1,0:T(4,128)(2,1)S(1)}, u32[]{:S(2)}, u32[]{:S(2)}) collective-permute-start(bf16[4,4096]{1,0:T(4,128)(2,1)S(1)} %slice.172), channel_id=1, source_target_pairs={{0,3},{1,0},{2,1},{3,2},{4,7},{5,4},{6,5},{7,6},{8,11},{9,8},{10,9... | collective-permute-start | bytes 98312 | tf_op jit(solution)/shard_map/ppermute | solution.py:62
  8.2 23.1 %copy-start.49 = (f32[1,1,32,8]{2,3,1,0:T(8,128)S(1)}, f32[1,1,32,8]{2,3,1,0:T(8,128)}, u32[]{:S(2)}) copy-start(f32[1,1,32,8]{2,3,1,0:T(8,128)} %param.10) | copy-start | bytes 3076
  8.2 23.1 %copy-start.53 = (s32[1,1,32]{2,1,0:T(1,128)S(1)}, s32[1,1,32]{2,1,0:T(1,128)}, u32[]{:S(2)}) copy-start(s32[1,1,32]{2,1,0:T(1,128)} %param.12) | copy-start | bytes 388
  8.2 23.2 %copy-start.48 = (s32[1,1,32,8]{2,3,1,0:T(8,128)S(1)}, s32[1,1,32,8]{2,3,1,0:T(8,128)}, u32[]{:S(2)}) copy-start(s32[1,1,32,8]{2,3,1,0:T(8,128)} %param.11) | copy-start | bytes 3076
  31.6 3.4 %collective-permute-start.2 = (bf16[4,4096]{1,0:T(4,128)(2,1)S(1)}, bf16[4,4096]{1,0:T(4,128)(2,1)S(1)}, u32[]{:S(2)}, u32[]{:S(2)}) collective-permute-start(bf16[4,4096]{1,0:T(4,128)(2,1)S(1)} %collective-permute-done), channel_id=1, source_target_pairs={{0,1},{1,2},{2,3},{3,0},{4,5},{5,6},{6,7},{7,4},{8,9},{9,10},{10,1... | collective-permute-start | bytes 98312 | tf_op jit(solution)/shard_map/ppermute | solution.py:54
  35.0 6.7 %collective-permute-start.3 = (bf16[1,1,16,4096]{3,2,1,0:T(8,128)(2,1)S(1)}, bf16[1,1,16,4096]{3,2,1,0:T(8,128)(2,1)S(1)}, u32[]{:S(2)}, u32[]{:S(2)}) collective-permute-start(bf16[1,1,16,4096]{3,2,1,0:T(8,128)(2,1)S(1)} %bitcast_dynamic-update-slice_fusion.6), channel_id=1, source_target_pairs={{0,16},{1,17},{2,18},{3,19},{4,20},{5,21},{6,22},{7,23},{8,24},{9,... | collective-permute-start | bytes 393224 | tf_op jit(solution)/shard_map/ppermute | solution.py:18
  39.2 6.9 %collective-permute-start.4 = (bf16[1,1,16,4096]{3,2,1,0:T(8,128)(2,1)S(1)}, bf16[1,1,16,4096]{3,2,1,0:T(8,128)(2,1)S(1)}, u32[]{:S(2)}, u32[]{:S(2)}) collective-permute-start(bf16[1,1,16,4096]{3,2,1,0:T(8,128)(2,1)S(1)} %bitcast_dynamic-update-slice_fusion.6), channel_id=1, source_target_pairs={{16,0},{17,1},{18,2},{19,3},{20,4},{21,5},{22,6},{23,7},{24,8},{25... | collective-permute-start | bytes 393224 | tf_op jit(solution)/shard_map/ppermute | solution.py:20
  46.1 9.9 %collective-permute-start.5 = (bf16[3,1,16,4096]{3,2,1,0:T(8,128)(2,1)S(1)}, bf16[3,1,16,4096]{3,2,1,0:T(8,128)(2,1)S(1)}, u32[]{:S(2)}, u32[]{:S(2)}) collective-permute-start(bf16[3,1,16,4096]{3,2,1,0:T(8,128)(2,1)S(1)} %pad_maximum_fusion.6), channel_id=1, source_target_pairs={{0,4},{4,8},{8,12},{1,5},{5,9},{9,13},{2,6},{6,10},{10,14},{3,7},{... | collective-permute-start | bytes 1179656 | tf_op jit(solution)/shard_map/ppermute | solution.py:18
  49.6 10.5 %collective-permute-start.6 = (bf16[3,1,16,4096]{3,2,1,0:T(8,128)(2,1)S(1)}, bf16[3,1,16,4096]{3,2,1,0:T(8,128)(2,1)S(1)}, u32[]{:S(2)}, u32[]{:S(2)}) collective-permute-start(bf16[3,1,16,4096]{3,2,1,0:T(8,128)(2,1)S(1)} %pad_maximum_fusion.6), channel_id=1, source_target_pairs={{4,0},{8,4},{12,8},{5,1},{9,5},{13,9},{6,2},{10,6},{14,10},{7,3},{... | collective-permute-start | bytes 1179656 | tf_op jit(solution)/shard_map/ppermute | solution.py:20
  64.5 8.7 %copy-start.24 = (bf16[32,64,1,64]{3,2,1,0:T(2,128)(2,1)S(1)}, bf16[32,64,1,64]{3,2,1,0:T(2,128)(2,1)}, u32[]{:S(2)}) copy-start(bf16[32,64,1,64]{3,2,1,0:T(2,128)(2,1)} %get-tuple-element.12) | copy-start | bytes 786436
  81.0 3.4 %collective-permute-start.7 = (bf16[4,4096]{1,0:T(4,128)(2,1)S(1)}, bf16[4,4096]{1,0:T(4,128)(2,1)S(1)}, u32[]{:S(2)}, u32[]{:S(2)}) collective-permute-start(bf16[4,4096]{1,0:T(4,128)(2,1)S(1)} %slice.197), channel_id=1, source_target_pairs={{0,1},{1,2},{2,3},{3,0},{4,5},{5,6},{6,7},{7,4},{8,9},{9,10},{10,1... | collective-permute-start | bytes 98312 | tf_op jit(solution)/shard_map/ppermute | solution.py:54
  81.1 3.4 %collective-permute-start.8 = (bf16[4,4096]{1,0:T(4,128)(2,1)S(1)}, bf16[4,4096]{1,0:T(4,128)(2,1)S(1)}, u32[]{:S(2)}, u32[]{:S(2)}) collective-permute-start(bf16[4,4096]{1,0:T(4,128)(2,1)S(1)} %slice.197), channel_id=1, source_target_pairs={{0,3},{1,0},{2,1},{3,2},{4,7},{5,4},{6,5},{7,6},{8,11},{9,8},{10,9... | collective-permute-start | bytes 98312 | tf_op jit(solution)/shard_map/ppermute | solution.py:62
  84.4 3.3 %collective-permute-start.9 = (bf16[4,4096]{1,0:T(4,128)(2,1)S(1)}, bf16[4,4096]{1,0:T(4,128)(2,1)S(1)}, u32[]{:S(2)}, u32[]{:S(2)}) collective-permute-start(bf16[4,4096]{1,0:T(4,128)(2,1)S(1)} %collective-permute-done.7), channel_id=1, source_target_pairs={{0,1},{1,2},{2,3},{3,0},{4,5},{5,6},{6,7},{7,4},{8,9},{9,10},{10,1... | collective-permute-start | bytes 98312 | tf_op jit(solution)/shard_map/ppermute | solution.py:54
  87.8 4.3 %collective-permute-start.10 = (bf16[1,1,16,4096]{3,2,1,0:T(8,128)(2,1)S(1)}, bf16[1,1,16,4096]{3,2,1,0:T(8,128)(2,1)S(1)}, u32[]{:S(2)}, u32[]{:S(2)}) collective-permute-start(bf16[1,1,16,4096]{3,2,1,0:T(8,128)(2,1)S(1)} %bitcast_dynamic-update-slice_fusion.3), channel_id=1, source_target_pairs={{0,16},{1,17},{2,18},{3,19},{4,20},{5,21},{6,22},{7,23},{8,24},{9,... | collective-permute-start | bytes 393224 | tf_op jit(solution)/shard_map/ppermute | solution.py:18
  89.6 6.9 %collective-permute-start.11 = (bf16[1,1,16,4096]{3,2,1,0:T(8,128)(2,1)S(1)}, bf16[1,1,16,4096]{3,2,1,0:T(8,128)(2,1)S(1)}, u32[]{:S(2)}, u32[]{:S(2)}) collective-permute-start(bf16[1,1,16,4096]{3,2,1,0:T(8,128)(2,1)S(1)} %bitcast_dynamic-update-slice_fusion.3), channel_id=1, source_target_pairs={{16,0},{17,1},{18,2},{19,3},{20,4},{21,5},{22,6},{23,7},{24,8},{25... | collective-permute-start | bytes 393224 | tf_op jit(solution)/shard_map/ppermute | solution.py:20
  96.5 8.9 %collective-permute-start.12 = (bf16[3,1,16,4096]{3,2,1,0:T(8,128)(2,1)S(1)}, bf16[3,1,16,4096]{3,2,1,0:T(8,128)(2,1)S(1)}, u32[]{:S(2)}, u32[]{:S(2)}) collective-permute-start(bf16[3,1,16,4096]{3,2,1,0:T(8,128)(2,1)S(1)} %pad_maximum_fusion.7), channel_id=1, source_target_pairs={{0,4},{4,8},{8,12},{1,5},{5,9},{9,13},{2,6},{6,10},{10,14},{3,7},{... | collective-permute-start | bytes 1179656 | tf_op jit(solution)/shard_map/ppermute | solution.py:18
  100.0 9.7 %collective-permute-start.13 = (bf16[3,1,16,4096]{3,2,1,0:T(8,128)(2,1)S(1)}, bf16[3,1,16,4096]{3,2,1,0:T(8,128)(2,1)S(1)}, u32[]{:S(2)}, u32[]{:S(2)}) collective-permute-start(bf16[3,1,16,4096]{3,2,1,0:T(8,128)(2,1)S(1)} %pad_maximum_fusion.7), channel_id=1, source_target_pairs={{4,0},{8,4},{12,8},{5,1},{9,5},{13,9},{6,2},{10,6},{14,10},{7,3},{... | collective-permute-start | bytes 1179656 | tf_op jit(solution)/shard_map/ppermute | solution.py:20
  114.0 7.1 %copy-start.4 = (bf16[32,64,1,64]{3,2,1,0:T(2,128)(2,1)S(1)}, bf16[32,64,1,64]{3,2,1,0:T(2,128)(2,1)}, u32[]{:S(2)}) copy-start(bf16[32,64,1,64]{3,2,1,0:T(2,128)(2,1)} %get-tuple-element.13) | copy-start | bytes 786436
  114.0 8.7 %copy-start.25 = (bf16[32,64,1,64]{3,2,1,0:T(2,128)(2,1)S(1)}, bf16[32,64,1,64]{3,2,1,0:T(2,128)(2,1)}, u32[]{:S(2)}) copy-start(bf16[32,64,1,64]{3,2,1,0:T(2,128)(2,1)} %get-tuple-element.12) | copy-start | bytes 786436
  114.0 8.7 %copy-start.43 = (f32[32]{0:T(128)S(1)}, f32[32]{0:T(128)}, u32[]{:S(2)}) copy-start(f32[32]{0:T(128)} %get-tuple-element.20) | copy-start | bytes 388
  130.5 23.3 %copy-start.54 = (f32[64]{0:T(128)S(1)}, f32[64]{0:T(128)}, u32[]{:S(2)}) copy-start(f32[64]{0:T(128)} %param.13) | copy-start | bytes 772
  130.5 23.9 %copy-start.27 = (f32[32,64,64]{2,1,0:T(8,128)S(1)}, f32[32,64,64]{2,1,0:T(8,128)}, u32[]{:S(2)}) copy-start(f32[32,64,64]{2,1,0:T(8,128)} %get-tuple-element.26) | copy-start | bytes 1572868
  131.9 3.4 %collective-permute-start.14 = (bf16[4,4096]{1,0:T(4,128)(2,1)S(1)}, bf16[4,4096]{1,0:T(4,128)(2,1)S(1)}, u32[]{:S(2)}, u32[]{:S(2)}) collective-permute-start(bf16[4,4096]{1,0:T(4,128)(2,1)S(1)} %slice.207), channel_id=1, source_target_pairs={{0,1},{1,2},{2,3},{3,0},{4,5},{5,6},{6,7},{7,4},{8,9},{9,10},{10,1... | collective-permute-start | bytes 98312 | tf_op jit(solution)/shard_map/ppermute | solution.py:54
  132.0 3.4 %collective-permute-start.15 = (bf16[4,4096]{1,0:T(4,128)(2,1)S(1)}, bf16[4,4096]{1,0:T(4,128)(2,1)S(1)}, u32[]{:S(2)}, u32[]{:S(2)}) collective-permute-start(bf16[4,4096]{1,0:T(4,128)(2,1)S(1)} %slice.207), channel_id=1, source_target_pairs={{0,3},{1,0},{2,1},{3,2},{4,7},{5,4},{6,5},{7,6},{8,11},{9,8},{10,9... | collective-permute-start | bytes 98312 | tf_op jit(solution)/shard_map/ppermute | solution.py:62
  135.3 3.3 %collective-permute-start.16 = (bf16[4,4096]{1,0:T(4,128)(2,1)S(1)}, bf16[4,4096]{1,0:T(4,128)(2,1)S(1)}, u32[]{:S(2)}, u32[]{:S(2)}) collective-permute-start(bf16[4,4096]{1,0:T(4,128)(2,1)S(1)} %collective-permute-done.14), channel_id=1, source_target_pairs={{0,1},{1,2},{2,3},{3,0},{4,5},{5,6},{6,7},{7,4},{8,9},{9,10},{10,1... | collective-permute-start | bytes 98312 | tf_op jit(solution)/shard_map/ppermute | solution.py:54
  138.7 4.2 %collective-permute-start.17 = (bf16[1,1,16,4096]{3,2,1,0:T(8,128)(2,1)S(1)}, bf16[1,1,16,4096]{3,2,1,0:T(8,128)(2,1)S(1)}, u32[]{:S(2)}, u32[]{:S(2)}) collective-permute-start(bf16[1,1,16,4096]{3,2,1,0:T(8,128)(2,1)S(1)} %bitcast_dynamic-update-slice_fusion), channel_id=1, source_target_pairs={{0,16},{1,17},{2,18},{3,19},{4,20},{5,21},{6,22},{7,23},{8,24},{9,... | collective-permute-start | bytes 393224 | tf_op jit(solution)/shard_map/ppermute | solution.py:18
  140.4 6.9 %collective-permute-start.18 = (bf16[1,1,16,4096]{3,2,1,0:T(8,128)(2,1)S(1)}, bf16[1,1,16,4096]{3,2,1,0:T(8,128)(2,1)S(1)}, u32[]{:S(2)}, u32[]{:S(2)}) collective-permute-start(bf16[1,1,16,4096]{3,2,1,0:T(8,128)(2,1)S(1)} %bitcast_dynamic-update-slice_fusion), channel_id=1, source_target_pairs={{16,0},{17,1},{18,2},{19,3},{20,4},{21,5},{22,6},{23,7},{24,8},{25... | collective-permute-start | bytes 393224 | tf_op jit(solution)/shard_map/ppermute | solution.py:20
  148.0 11.4 %collective-permute-start.19 = (bf16[3,1,16,4096]{3,2,1,0:T(8,128)(2,1)}, bf16[3,1,16,4096]{3,2,1,0:T(8,128)(2,1)}, u32[]{:S(2)}, u32[]{:S(2)}) collective-permute-start(bf16[3,1,16,4096]{3,2,1,0:T(8,128)(2,1)} %pad_maximum_fusion.8), channel_id=1, source_target_pairs={{0,4},{4,8},{8,12},{1,5},{5,9},{9,13},{2,6},{6,10},{10,14},{3,7},{... | collective-permute-start | bytes 1179656 | tf_op jit(solution)/shard_map/ppermute | solution.py:18
  152.2 10.8 %collective-permute-start.20 = (bf16[3,1,16,4096]{3,2,1,0:T(8,128)(2,1)}, bf16[3,1,16,4096]{3,2,1,0:T(8,128)(2,1)}, u32[]{:S(2)}, u32[]{:S(2)}) collective-permute-start(bf16[3,1,16,4096]{3,2,1,0:T(8,128)(2,1)} %pad_maximum_fusion.8), channel_id=1, source_target_pairs={{4,0},{8,4},{12,8},{5,1},{9,5},{13,9},{6,2},{10,6},{14,10},{7,3},{... | collective-permute-start | bytes 1179656 | tf_op jit(solution)/shard_map/ppermute | solution.py:20
  168.5 8.7 %copy-start.26 = (bf16[32,64,1,64]{3,2,1,0:T(2,128)(2,1)S(1)}, bf16[32,64,1,64]{3,2,1,0:T(2,128)(2,1)}, u32[]{:S(2)}) copy-start(bf16[32,64,1,64]{3,2,1,0:T(2,128)(2,1)} %get-tuple-element.12) | copy-start | bytes 786436
  168.5 8.7 %copy-start.44 = (f32[32]{0:T(128)S(1)}, f32[32]{0:T(128)}, u32[]{:S(2)}) copy-start(f32[32]{0:T(128)} %get-tuple-element.20) | copy-start | bytes 388
  (44 other events, 77.3 us)
